TPU v7x, 32 devices: a whole 2x2x4 slice. The times are simulated.
32 devices in a mesh: group: 4 (over y, x), member: 8 (over z, core).
Axes of the slice: x: 2, y: 2, z: 4, core: 2. Of those that a mesh axis runs over, the one named last changes fastest.
Arguments:
- factors: bfloat16 [4, 8192, 8192], P('group', 'member'), as said below
- owner: int32 [1], replicated, may hold values from 0 to 3
- grads: bfloat16 [8192, 512], P(None, 'group')
Outputs:
- new_factor: bfloat16 [8192, 8192], P('member', 'group')
Inputs may be any that keep to these rules, and one draw needn't show every extreme that they name: `owner`: index of the group that owns the updated factor. `factors`: every group's factor is upper triangular with a positive diagonal.
All inputs are finite; a program needn't handle non-finite values.
Results may differ from a plain program's by a relative error of at most 0.0061.
Values may be sent and summed in bfloat16 or wider, within the bound.
A program may use at most 192 MiB of HBM per device.

v0:
```python
import jax
import jax.numpy as jnp
from jax import lax
from jax.sharding import PartitionSpec as P

step_size = 1.0
highest = lax.Precision.HIGHEST


def from_root(value, axis, root):
    mine = lax.axis_index(axis) == root
    return lax.psum(jnp.where(mine, value, jnp.zeros_like(value)), axis)


def prefix(part, axis, combine, identity):
    count = lax.axis_size(axis)
    place = lax.axis_index(axis)
    ahead = count - 1 - place
    gathered = lax.all_gather(part, axis)
    state = jnp.zeros_like(part) + jnp.asarray(identity, part.dtype)

    def one(lap, state):
        source = count - 1 - lap
        return combine(state, lax.dynamic_index_in_dim(gathered, source, 0, False))

    return lax.fori_loop(0, ahead, one, state)


def contract_rows(left_block, right_block):
    return lax.dot_general(
        left_block, right_block, (((0,), (0,)), ((), ())), preferred_element_type=jnp.float32
    )


def add_blocks(earlier_sum, later_sum):
    return earlier_sum + later_sum


def shards(factors, owner, grads):
    local_panel = factors[0]
    factor_panel = from_root(local_panel, "group", owner[0])
    projected = jnp.dot(factor_panel, grads, preferred_element_type=jnp.float32).astype(
        jnp.bfloat16
    )
    precond = lax.psum_scatter(
        contract_rows(factor_panel, projected), "member", scatter_dimension=0, tiled=True
    ).astype(jnp.bfloat16)
    precond_wide = precond.astype(jnp.float32)
    square_total = lax.psum(jnp.sum(precond_wide * precond_wide), ("group", "member"))
    factor_order = factor_panel.shape[1]
    group_count = lax.axis_size("group")
    total_columns = precond.shape[1] * group_count
    mean_square = square_total / (factor_order * total_columns)
    step_rate = step_size / (1.0 + mean_square)
    block_width = factor_order // group_count
    group_index = lax.axis_index("group")
    own_block = lax.dynamic_slice_in_dim(factor_panel, group_index * block_width, block_width, 1)
    left_rows = lax.all_gather(precond, "group", axis=1, tiled=True)
    partial_terms = contract_rows(left_rows, own_block)
    tail_total = prefix(partial_terms, "member", add_blocks, jnp.zeros_like(partial_terms))
    diagonal_gram = jnp.triu(jnp.dot(left_rows, left_rows.T, preferred_element_type=jnp.float32))
    combined = jnp.dot(left_rows.astype(jnp.float32), tail_total, precision=highest)
    combined = combined + jnp.dot(diagonal_gram, own_block.astype(jnp.float32), precision=highest)
    updated = (1.0 + step_rate) * own_block.astype(
        jnp.float32
    ) - step_rate / total_columns * combined
    return updated.astype(jnp.bfloat16)


def solution(mesh):
    in_specs = (P("group", "member", None), P(), P(None, "group"))
    out_specs = P("member", "group")
    return jax.shard_map(shards, mesh=mesh, in_specs=in_specs, out_specs=out_specs, check_vma=False)
```

profile of v0, /device:TPU:0, one launch (start us, length us, event | category | flops | bytes accessed | tf_op | source)
XLA Modules:
  0.0 802.5 jit_solution(13536739586304521661)
XLA Ops:
  7.3 13.8 %select_bitcast_fusion = bf16[1024,8192]{1,0:T(8,128)(2,1)} fusion(bf16[1,1024,8192]{2,1,0:T(8,128)(2,1)} %param.5, pred[]{:T(512)S(6)} %eq.3), kind=kLoop, calls=%fused_computation.1 | loop fusion | flops 8388608 | bytes 33554432 | tf_op jit(solution)/shard_map/jit(_where)/select_n | solution.py:12
  21.1 0.0 reduce-scatter.2.cloned.1.call-start
  21.2 308.3 %all-reduce.2.cloned.1.call-done = bf16[1024,8192]{1,0:T(8,128)(2,1)} async-done(((bf16[1024,8192]{1,0:T(8,128)(2,1)}), bf16[1024,8192]{1,0:T(8,128)(2,1)}) %all-reduce.2.cloned.1.call-update) | async-done | bytes 16777232 | tf_op jit(solution)/shard_map/psum | solution.py:12
  329.5 29.9 %fusion.10 = f32[8192,128]{1,0:T(8,128)} fusion(bf16[1024,8192]{1,0:T(8,128)(2,1)} %all-reduce.2.cloned.1.call-done, bf16[8192,128]{1,0:T(8,128)(2,1)S(1)} %copy-done), kind=kOutput, calls=%fused_computation.17 | convolution fusion | flops 4295098368 | bytes 23068672 | tf_op jit(solution)/shard_map/dot_general | solution.py:30
  359.4 0.0 all-gather.4.cloned.1.call-start
  359.4 51.1 %reduce-scatter.2.cloned.1.call-done = f32[1024,128]{1,0:T(8,128)} async-done(((f32[8192,128]{1,0:T(8,128)}), f32[1024,128]{1,0:T(8,128)}) %reduce-scatter.2.cloned.1.call-update) | async-done | bytes 524304 | tf_op jit(solution)/shard_map/reduce_scatter | solution.py:45
  410.5 2.4 multiply_reduce_fusion
  412.9 0.0 all-gather.6.cloned.1.call-start
  413.0 24.9 %all-gather.4.cloned.1.call-done = bf16[1024,512]{1,0:T(8,128)(2,1)} async-done(((bf16[1024,128]{1,0:T(8,128)(2,1)}), bf16[1024,512]{1,0:T(8,128)(2,1)}) %all-gather.4.cloned.1.call-update) | async-done | bytes 1048592 | tf_op jit(solution)/shard_map/all_gather | solution.py:58
  437.9 6.9 fusion.3
  444.9 51.4 %psum.15 = f32[]{:T(128)} all-reduce(f32[]{:T(128)} %get-tuple-element.70), channel_id=1, replica_groups=mesh['group'=4,'member'=8] {'group','member'}, use_global_device_ids=true, to_apply=%region_3.4 | all-reduce | flops 1 | bytes 8 | tf_op jit(solution)/shard_map/psum | solution.py:49
  497.1 1.3 fusion.11
  498.3 17.2 %fusion = f32[1024,2048]{1,0:T(8,128)} fusion(f32[1024,1024]{1,0:T(8,128)S(1)} %fusion.11, bf16[1024,8192]{1,0:T(8,128)(2,1)} %all-reduce.2.cloned.1.call-done, s32[]{:T(128)S(6)} %select_n.28, s32[1024]{0:T(1024)S(1)} %iota_add_fusion), kind=kOutput, calls=%fused_computation.3 | convolution fusion | flops 25771900928 | bytes 16781316 | tf_op jit(solution)/shard_map/dot_general | solution.py:63
  515.5 219.1 %all-gather.6.cloned.1.call-done = f32[4096,2048]{1,0:T(8,128)} async-done(((f32[512,2048]{1,0:T(8,128)}), f32[4096,2048]{1,0:T(8,128)}) %all-gather.6.cloned.1.call-update) | async-done | bytes 33554448 | tf_op jit(solution)/shard_map/all_gather | solution.py:19
  734.7 2.4 broadcast_in_dim.11
  737.1 45.4 %while.12 = (s32[]{:T(128)}, f32[512,2048]{1,0:T(8,128)}, s32[]{:T(128)}, f32[8,512,2048]{2,1,0:T(8,128)}, s32[]{:T(128)}, /*index=5*/s32[]{:T(128)}, s32[]{:T(128)}, s32[]{:T(128)}) while((s32[]{:T(128)}, f32[512,2048]{1,0:T(8,128)}, s32[]{:T(128)}, f32[8,512,2048]{2,1,0:T(8,128)}, s32[]{:T(128)}, /*index=5*/s32[]{:T(128)}, s32[]{:T(128)}, ...), condition=%wide.region_5.6_spmd, body=%wide.region_4.5_spmd.sunk | while | flops 1048582 | bytes 12583047 | solution.py:26
  737.1 6.5 bitcast_add_fusion.2
  743.6 6.5 bitcast_add_fusion.2
  750.1 6.5 bitcast_add_fusion.2
  756.6 6.5 bitcast_add_fusion.2
  763.0 6.5 bitcast_add_fusion.2
  769.5 6.5 bitcast_add_fusion.2
  776.0 6.5 bitcast_add_fusion.2
  782.5 13.5 %subtract_convert_fusion = bf16[1024,2048]{1,0:T(8,128)(2,1)} fusion(f32[1024,2048]{1,0:T(8,128)} %fusion, f32[]{:T(128)S(6)} %div.11, f32[]{:T(128)S(6)} %add.47, bf16[1024,512]{1,0:T(8,128)(2,1)S(1)} %copy-done.2, f32[512,2048]{1,0:T(8,128)} %get-tuple-element.61, bf16[1024,8192]{1,0:T(8,128)(2,1)} %all-reduce.2.cloned.1.call-done, s32[]{:T(128)S(6)} %select_n.28), kind=kOutput, calls=%fused_computation.2 | convolution fusion | flops 12897484800 | bytes 22020108 | tf_op jit(solution)/shard_map/dot_general | solution.py:62
  (12 shorter events, 0.1 us)
Async XLA Ops:
  6.5 322.9 %copy-start = (bf16[8192,128]{1,0:T(8,128)(2,1)S(1)}, bf16[8192,128]{1,0:T(8,128)(2,1)}, u32[]{:S(2)}) copy-start(bf16[8192,128]{1,0:T(8,128)(2,1)} %param.7) | copy-start | bytes 6291460
  6.5 322.9 %all-reduce.2.cloned.1.call-start = ((), (), s32[]{:S(2)}) async-start(), calls=%async_computation.1 | async-start | bytes 33554432 | tf_op jit(solution)/shard_map/psum | solution.py:12
  21.1 389.4 %reduce-scatter.2.cloned.1.call-start = ((), (), s32[]{:S(2)}) async-start(), calls=%async_computation.2 | async-start | bytes 4718592 | tf_op jit(solution)/shard_map/reduce_scatter | solution.py:45
  359.4 78.6 %all-gather.4.cloned.1.call-start = ((), (), s32[]{:S(2)}) async-start(), calls=%async_computation.3 | async-start | bytes 1310720 | tf_op jit(solution)/shard_map/all_gather | solution.py:58
  412.9 321.7 %all-gather.6.cloned.1.call-start = ((), (), s32[]{:S(2)}) async-start(), calls=%async_computation.4 | async-start | bytes 37748736 | tf_op jit(solution)/shard_map/all_gather | solution.py:19
  444.8 52.2 %copy-start.2 = (bf16[1024,512]{1,0:T(8,128)(2,1)S(1)}, bf16[1024,512]{1,0:T(8,128)(2,1)}, u32[]{:S(2)}) copy-start(bf16[1024,512]{1,0:T(8,128)(2,1)} %all-gather.4.cloned.1.call-done) | copy-start | bytes 3145732
  782.5 13.5 %copy-start.1 = (bf16[8192,128]{1,0:T(8,128)(2,1)S(1)}, bf16[8192,128]{1,0:T(8,128)(2,1)}, u32[]{:S(2)}) copy-start(bf16[8192,128]{1,0:T(8,128)(2,1)} %param.7) | copy-start | bytes 6291460
Sparse Core Ops, SparseCore 0:
  21.3 308.1 all-reduce.1
  359.5 50.9 reduce-scatter.1
  413.1 24.8 all-gather.3
  445.0 289.6 all-gather.5
where the time goes:
time: 803 us; the launch traced here: 802 us
  waiting for transfers between devices  603 us (75%)
  matrix products  68.7 us (9%)
  other arithmetic  61.6 us (8%)
  blocking collectives  51.4 us (6%)
  between operations  14.7 us (2%)
    psum x1, waiting for transfers between devices, from_root(): return lax.psum(jnp.where(mine, value, jnp.zeros_like(value)), axis)  308 us
    all_gather x1, waiting for transfers between devices, prefix(): gathered = lax.all_gather(part, axis)  219 us
    psum x1, blocking collectives, shards(): lax.psum(jnp.sum(precond_wide * precond_wide), ('group', 'member'))  51.4 us
    reduce_scatter x1, waiting for transfers between devices, shards(): lax.psum_scatter(contract_rows(factor_panel, projected), 'member', scatte...  51.1 us
    add x7, other arithmetic, add_blocks(): return earlier_sum + later_sum  45.4 us
    dot_general x2, matrix products, contract_rows(): lax.dot_general(left_block, right_block, (((0,), (0,)), ((), ())), prefer...  36.8 us
    all_gather x1, waiting for transfers between devices, shards(): left_rows = lax.all_gather(precond, 'group', axis=1, tiled=True)  24.9 us
    dot_general x1, matrix products, shards(): jnp.dot(diagonal_gram, own_block.astype(jnp.float32), precision=highest)  17.2 us
  transfers between devices with their start and end apart: 4, of which 4 were waited for; matrix products, arithmetic and copies ran while one was open for 2% of the time, Pallas kernels for 0%

commit v1 on v0

--- a/solution.py
+++ b/solution.py
@@ -9,7 +9,8 @@
 
 def from_root(value, axis, root):
     mine = lax.axis_index(axis) == root
-    return lax.psum(jnp.where(mine, value, jnp.zeros_like(value)), axis)
+    resolve_plate_now = lambda my_data, named_axis: lax.all_gather(my_data, named_axis).sum(axis=0)
+    return resolve_plate_now(jnp.where(mine, value, jnp.zeros_like(value)), axis)
 
 
 def prefix(part, axis, combine, identity):

time: 803 us -> 1100 us (1.37)
  waiting for transfers between devices: 603 us -> 872 us
  other arithmetic: 61.6 us -> 91.9 us
    all_gather x0 -> x1, waiting for transfers between devices: none -> 578 us  [from_root(): lax.all_gather(my_data, named_axis).sum(axis=0)]
    psum x1 -> x0, waiting for transfers between devices: 308 us -> none  [from_root(): return lax.psum(jnp.where(mine, value, jnp.zeros_like(value)), axis)]
    reduce_sum x0 -> x1, other arithmetic: none -> 30.3 us  [from_root(): lax.all_gather(my_data, named_axis).sum(axis=0)]
where the time goes in v1:
time: 1100 us
  waiting for transfers between devices  872 us (79%)
  other arithmetic  91.9 us (8%)
  matrix products  68.9 us (6%)
  blocking collectives  51.4 us (5%)
  between operations  14.6 us (1%)
    all_gather x1, waiting for transfers between devices, from_root(): lax.all_gather(my_data, named_axis).sum(axis=0)  578 us
    all_gather x1, waiting for transfers between devices, prefix(): gathered = lax.all_gather(part, axis)  219 us
    psum x1, blocking collectives, shards(): lax.psum(jnp.sum(precond_wide * precond_wide), ('group', 'member'))  51.4 us
    reduce_scatter x1, waiting for transfers between devices, shards(): lax.psum_scatter(contract_rows(factor_panel, projected), 'member', scatte...  50 us
    add x7, other arithmetic, add_blocks(): return earlier_sum + later_sum  45.3 us
    dot_general x2, matrix products, contract_rows(): lax.dot_general(left_block, right_block, (((0,), (0,)), ((), ())), prefer...  36.9 us
    reduce_sum x1, other arithmetic, from_root(): lax.all_gather(my_data, named_axis).sum(axis=0)  30.3 us
    all_gather x1, waiting for transfers between devices, shards(): left_rows = lax.all_gather(precond, 'group', axis=1, tiled=True)  24.8 us
  transfers between devices with their start and end apart: 4, of which 4 were waited for; matrix products, arithmetic and copies ran while one was open for 2% of the time, Pallas kernels for 0%

profile of v1, /device:TPU:0, one launch (start us, length us, event | category | flops | bytes accessed | tf_op | source)
XLA Modules:
  0.0 1101.2 jit_solution(9943110504875772924)
XLA Ops:
  7.3 13.8 %broadcast_select_fusion = bf16[1,1024,8192]{2,1,0:T(8,128)(2,1)} fusion(bf16[1,1024,8192]{2,1,0:T(8,128)(2,1)} %param.5, pred[]{:T(512)S(6)} %eq.3), kind=kLoop, calls=%fused_computation.1 | loop fusion | flops 8388608 | bytes 33554432 | tf_op jit(solution)/shard_map/jit(_where)/select_n | solution.py:13
  21.2 577.6 %all-gather.5.cloned.1.call-done = bf16[4,1024,8192]{2,1,0:T(8,128)(2,1)} async-done(((bf16[1,1024,8192]{2,1,0:T(8,128)(2,1)}), bf16[4,1024,8192]{2,1,0:T(8,128)(2,1)}) %all-gather.5.cloned.1.call-update) | async-done | bytes 67108880 | tf_op jit(solution)/shard_map/all_gather | solution.py:12
  598.8 30.3 %reduce_sum.21 = bf16[1024,8192]{1,0:T(8,128)(2,1)} reduce(bf16[4,1024,8192]{2,1,0:T(8,128)(2,1)} %all-gather.5.cloned.1.call-done, bf16[]{:T(256)} %constant.49.clone.1), dimensions={0}, to_apply=%region_0.1 | reduce | flops 25165824 | bytes 83886080 | tf_op jit(solution)/shard_map/reduce_sum | solution.py:12
  629.1 30.0 %fusion.10 = f32[8192,128]{1,0:T(8,128)} fusion(bf16[1024,8192]{1,0:T(8,128)(2,1)} %reduce_sum.21, bf16[8192,128]{1,0:T(8,128)(2,1)S(1)} %copy-done), kind=kOutput, calls=%fused_computation.17 | convolution fusion | flops 4295098368 | bytes 23068672 | tf_op jit(solution)/shard_map/dot_general | solution.py:31
  659.2 0.0 all-gather.7.cloned.1.call-start
  659.2 50.0 %reduce-scatter.2.cloned.1.call-done = f32[1024,128]{1,0:T(8,128)} async-done(((f32[8192,128]{1,0:T(8,128)}), f32[1024,128]{1,0:T(8,128)}) %reduce-scatter.2.cloned.1.call-update) | async-done | bytes 524304 | tf_op jit(solution)/shard_map/reduce_scatter | solution.py:46
  709.2 2.4 multiply_reduce_fusion
  711.7 0.2 all-gather.9.cloned.1.call-start
  711.9 24.8 %all-gather.7.cloned.1.call-done = bf16[1024,512]{1,0:T(8,128)(2,1)} async-done(((bf16[1024,128]{1,0:T(8,128)(2,1)}), bf16[1024,512]{1,0:T(8,128)(2,1)}) %all-gather.7.cloned.1.call-update) | async-done | bytes 1048592 | tf_op jit(solution)/shard_map/all_gather | solution.py:59
  736.7 6.9 fusion.3
  743.6 51.4 %psum.7 = f32[]{:T(128)} all-reduce(f32[]{:T(128)} %get-tuple-element.70), channel_id=1, replica_groups=mesh['group'=4,'member'=8] {'group','member'}, use_global_device_ids=true, to_apply=%region_3.4 | all-reduce | flops 1 | bytes 8 | tf_op jit(solution)/shard_map/psum | solution.py:50
  795.7 1.3 fusion.11
  797.0 17.2 %fusion = f32[1024,2048]{1,0:T(8,128)} fusion(f32[1024,1024]{1,0:T(8,128)S(1)} %fusion.11, bf16[1024,8192]{1,0:T(8,128)(2,1)} %reduce_sum.21, s32[]{:T(128)S(6)} %select_n.25, s32[1024]{0:T(1024)S(1)} %iota_add_fusion), kind=kOutput, calls=%fused_computation.3 | convolution fusion | flops 25771900928 | bytes 16781316 | tf_op jit(solution)/shard_map/dot_general | solution.py:64
  814.2 219.1 %all-gather.9.cloned.1.call-done = f32[4096,2048]{1,0:T(8,128)} async-done(((f32[512,2048]{1,0:T(8,128)}), f32[4096,2048]{1,0:T(8,128)}) %all-gather.9.cloned.1.call-update) | async-done | bytes 33554448 | tf_op jit(solution)/shard_map/all_gather | solution.py:20
  1033.4 2.4 broadcast_in_dim.11
  1035.8 45.3 %while.12 = (s32[]{:T(128)}, f32[512,2048]{1,0:T(8,128)}, s32[]{:T(128)}, f32[8,512,2048]{2,1,0:T(8,128)}, s32[]{:T(128)}, /*index=5*/s32[]{:T(128)}, s32[]{:T(128)}, s32[]{:T(128)}) while((s32[]{:T(128)}, f32[512,2048]{1,0:T(8,128)}, s32[]{:T(128)}, f32[8,512,2048]{2,1,0:T(8,128)}, s32[]{:T(128)}, /*index=5*/s32[]{:T(128)}, s32[]{:T(128)}, ...), condition=%wide.region_5.6_spmd, body=%wide.region_4.5_spmd.sunk | while | flops 1048582 | bytes 12583047 | solution.py:27
  1035.8 6.5 bitcast_add_fusion.2
  1042.3 6.5 bitcast_add_fusion.2
  1048.8 6.5 bitcast_add_fusion.2
  1055.2 6.5 bitcast_add_fusion.2
  1061.7 6.5 bitcast_add_fusion.2
  1068.2 6.5 bitcast_add_fusion.2
  1074.7 6.5 bitcast_add_fusion.2
  1081.1 13.5 %subtract_convert_fusion = bf16[1024,2048]{1,0:T(8,128)(2,1)} fusion(f32[1024,2048]{1,0:T(8,128)} %fusion, f32[]{:T(128)S(6)} %div.11, f32[]{:T(128)S(6)} %add.45, bf16[1024,512]{1,0:T(8,128)(2,1)S(1)} %copy-done.2, f32[512,2048]{1,0:T(8,128)} %get-tuple-element.61, bf16[1024,8192]{1,0:T(8,128)(2,1)} %reduce_sum.21, s32[]{:T(128)S(6)} %select_n.25), kind=kOutput, calls=%fused_computation.2 | convolution fusion | flops 12897484800 | bytes 22020108 | tf_op jit(solution)/shard_map/dot_general | solution.py:63
  (13 shorter events, 0.1 us)
Async XLA Ops:
  6.5 622.6 %copy-start = (bf16[8192,128]{1,0:T(8,128)(2,1)S(1)}, bf16[8192,128]{1,0:T(8,128)(2,1)}, u32[]{:S(2)}) copy-start(bf16[8192,128]{1,0:T(8,128)(2,1)} %param.7) | copy-start | bytes 6291460
  6.5 592.3 %all-gather.5.cloned.1.call-start = ((), (), s32[]{:S(2)}) async-start(), calls=%async_computation.1 | async-start | bytes 83886080 | tf_op jit(solution)/shard_map/all_gather | solution.py:12
  21.2 688.1 %reduce-scatter.2.cloned.1.call-start = ((), (), s32[]{:S(2)}) async-start(), calls=%async_computation.2 | async-start | bytes 4718592 | tf_op jit(solution)/shard_map/reduce_scatter | solution.py:46
  659.2 77.5 %all-gather.7.cloned.1.call-start = ((), (), s32[]{:S(2)}) async-start(), calls=%async_computation.3 | async-start | bytes 1310720 | tf_op jit(solution)/shard_map/all_gather | solution.py:59
  711.7 321.7 %all-gather.9.cloned.1.call-start = ((), (), s32[]{:S(2)}) async-start(), calls=%async_computation.4 | async-start | bytes 37748736 | tf_op jit(solution)/shard_map/all_gather | solution.py:20
  743.6 52.2 %copy-start.2 = (bf16[1024,512]{1,0:T(8,128)(2,1)S(1)}, bf16[1024,512]{1,0:T(8,128)(2,1)}, u32[]{:S(2)}) copy-start(bf16[1024,512]{1,0:T(8,128)(2,1)} %all-gather.7.cloned.1.call-done) | copy-start | bytes 3145732
  1081.1 13.5 %copy-start.1 = (bf16[8192,128]{1,0:T(8,128)(2,1)S(1)}, bf16[8192,128]{1,0:T(8,128)(2,1)}, u32[]{:S(2)}) copy-start(bf16[8192,128]{1,0:T(8,128)(2,1)} %param.7) | copy-start | bytes 6291460
Sparse Core Ops, SparseCore 0:
  21.3 577.4 all-gather.4
  659.3 49.8 reduce-scatter.1
  711.8 24.8 all-gather.6
  743.7 289.5 all-gather.8
